TPU v7x, 256 devices: a whole 4x4x8 slice. The times are simulated.
256 devices in a mesh: wide: 32 (over x, y, core), narrow: 8 (over z).
Axes of the slice: x: 4, y: 4, z: 8, core: 2. Of those that a mesh axis runs over, the one named last changes fastest.
Arguments:
- sources: float32 [32, 8, 16, 2, 512], P('wide', 'narrow'), may hold values from -6 to 6
- schur_blocks: bfloat16 [32, 8, 2048, 2048], P('wide', 'narrow'), as said below
- scaling: float32 [32, 8, 2, 512], P('wide', 'narrow'), may hold values from 0.08 to 0.4
- coarse_basis: float32 [32, 8, 2, 2, 8, 512], P('wide', 'narrow'), may hold values from -0.09375 to 0.09375
- coarse_inverse: float32 [32, 80, 80], P('wide'), as said below
- face_sizes: int32 [32, 8, 2], P('wide', 'narrow'), may hold values from 0 to 512, as said below
- face_match: int32 [32, 8, 2, 512], P('wide', 'narrow'), may hold values from 0 to 511, as said below
- face_slots: int32 [32, 8, 4], P('wide', 'narrow'), may hold values from 0 to 3, each once within a row
- corner_slots: int32 [33, 9], replicated, may hold values from 0 to 319, as said below
Outputs:
- solution: float32 [32, 8, 16, 2, 512], P('wide', 'narrow')
- residual: float32 [32, 8, 16, 2, 512], P('wide', 'narrow')
Inputs may be any that keep to these rules, and one draw needn't show every extreme that they name: `face_sizes`: the east faces of the last wide index and the north faces of the last narrow index have 0 unknowns; every other face has 128 to 512, and some face has exactly 512. `face_match`: each block is a permutation of 0 to 511 that maps the positions below the size of the matching owned face onto themselves. `corner_slots`: distinct slots for distinct vertices; slot 319 is used. `schur_blocks`: each block is symmetric and positive definite. `coarse_inverse`: each block is symmetric and positive definite.
All inputs are finite; a program needn't handle non-finite values.
Results may differ from a plain program's by a relative error of at most 0.0052.
Values may be sent and summed in bfloat16 or wider, within the bound.
A program may use at most 64 MiB of HBM per device.

v0:
```python
import jax
import jax.numpy as jnp
from jax import lax
from jax.sharding import PartitionSpec as P

ITERS = 2
highest = lax.Precision.HIGHEST


def shifted(block, axis, distance):
    devices = range(lax.axis_size(axis))
    route = [(i - distance, i) for i in devices if i - distance in devices]
    return lax.ppermute(block, axis, route)


def body(
    sources,
    schur_blocks,
    scaling,
    coarse_basis,
    coarse_inverse,
    face_sizes,
    face_match,
    face_slots,
    corner_slots,
):
    wide_count = lax.axis_size("wide")
    wide_at = lax.axis_index("wide")
    narrow_at = lax.axis_index("narrow")
    nrhs_count = sources.shape[2]
    face_width = sources.shape[4]
    basis_count = coarse_basis.shape[4]
    block_order = coarse_inverse.shape[1]
    capacity = block_order // basis_count
    slot_count = capacity * wide_count
    places = lax.broadcasted_iota(jnp.int32, (2, face_width), 1)
    live_mask = (places < face_sizes[0, 0][:, None]).astype(jnp.float32)
    weights = scaling[0, 0] * live_mask
    vectors = coarse_basis[0, 0] * live_mask[:, None, None, :]
    forward = face_match[0, 0]
    source_rows = lax.broadcasted_iota(jnp.int32, (2, face_width, face_width), 1)
    match_table = (forward[:, None, :] == source_rows).astype(jnp.float32)
    match_narrow = match_table.astype(jnp.bfloat16)
    slot_table = (face_slots[0, 0][:, None] == jnp.arange(4, dtype=jnp.int32)[None, :]).astype(
        jnp.float32
    )
    matrix = schur_blocks[0, 0]
    square = lax.dynamic_slice(corner_slots, (wide_at, narrow_at), (2, 2))
    corner_ids = jnp.stack([square[1, 0], square[1, 1], square[0, 1], square[1, 1]])
    incidence = (corner_ids[:, None] == jnp.arange(slot_count, dtype=jnp.int32)[None, :]).astype(
        jnp.float32
    )
    inverse_block = coarse_inverse[0]
    initial = sources[0, 0] * live_mask[None]

    def finish(residual, solved_slots):
        local_values = jnp.dot(
            incidence, solved_slots, precision=highest, preferred_element_type=jnp.float32
        )
        local_values = local_values.reshape(2, 2, basis_count, nrhs_count)
        return weights[None] * residual + jnp.einsum(
            "femk,femr->rfk", vectors, local_values, precision=highest
        )

    def precondition(residual):
        partial_value = jnp.einsum("femk,rfk->femr", vectors, residual, precision=highest).reshape(
            4, basis_count * nrhs_count
        )
        dense_part = jnp.dot(
            incidence.T, partial_value, precision=highest, preferred_element_type=jnp.float32
        )
        owned_rows = lax.psum_scatter(dense_part, "wide", scatter_dimension=0, tiled=True)
        owner_block = lax.psum(owned_rows, "narrow").reshape(block_order, nrhs_count)
        solved = jnp.dot(
            inverse_block, owner_block, precision=highest, preferred_element_type=jnp.float32
        )
        all_solved = lax.all_gather(
            solved.reshape(capacity, basis_count * nrhs_count), "wide", axis=0, tiled=True
        )
        precond = finish(residual, all_solved)
        inner_value = lax.psum(jnp.sum(residual * precond, axis=(1, 2)), ("wide", "narrow"))
        return (precond, inner_value)

    residual = initial
    solution = jnp.zeros_like(initial)
    precond, inner_now = precondition(residual)
    direction = precond
    for iteration in range(ITERS):
        rounded = direction.astype(jnp.bfloat16)
        from_west = shifted(rounded[:, 0], "wide", 1)
        from_south = shifted(rounded[:, 1], "narrow", 1)
        west_face = jnp.dot(from_west, match_narrow[0], preferred_element_type=jnp.float32)
        south_face = jnp.dot(from_south, match_narrow[1], preferred_element_type=jnp.float32)
        stacked = jnp.stack(
            [
                rounded[:, 0].astype(jnp.float32),
                rounded[:, 1].astype(jnp.float32),
                west_face,
                south_face,
            ],
            axis=1,
        )
        slotted = jnp.einsum("rdk,ds->rsk", stacked, slot_table, precision=highest).astype(
            jnp.bfloat16
        )
        product = jnp.dot(
            slotted.reshape(nrhs_count, 4 * face_width), matrix, preferred_element_type=jnp.float32
        )
        by_face = jnp.einsum(
            "rsk,ds->rdk", product.reshape(nrhs_count, 4, face_width), slot_table, precision=highest
        )
        to_west = jnp.einsum("rk,mk->rm", by_face[:, 2], match_table[0], precision=highest)
        to_south = jnp.einsum("rk,mk->rm", by_face[:, 3], match_table[1], precision=highest)
        from_east = shifted(to_west, "wide", -1)
        from_north = shifted(to_south, "narrow", -1)
        summed_all = jnp.stack([by_face[:, 0] + from_east, by_face[:, 1] + from_north], axis=1)
        applied = summed_all * live_mask[None]
        curvature = lax.psum(jnp.sum(direction * applied, axis=(1, 2)), ("wide", "narrow"))
        step_size = inner_now / curvature
        solution = solution + step_size[:, None, None] * direction
        residual = residual - step_size[:, None, None] * applied
        if iteration + 1 < ITERS:
            precond, inner_new = precondition(residual)
            direction = precond + (inner_new / inner_now)[:, None, None] * direction
            inner_now = inner_new
    return (solution[None, None], residual[None, None])


def solution(mesh):
    placed = (
        P("wide", "narrow", None, None, None),
        P("wide", "narrow", None, None),
        P("wide", "narrow", None, None),
        P("wide", "narrow", None, None, None, None),
        P("wide", None, None),
        P("wide", "narrow", None),
        P("wide", "narrow", None, None),
        P("wide", "narrow", None),
        P(),
    )
    return jax.shard_map(
        body,
        mesh=mesh,
        in_specs=placed,
        out_specs=(P("wide", "narrow", None, None, None), P("wide", "narrow", None, None, None)),
        check_vma=False,
    )
```

profile of v0, /device:TPU:1, one launch (start us, length us, event | category | flops | bytes accessed | tf_op | source)
XLA Modules:
  0.0 640.1 jit_solution(5082868968421109135)
XLA Ops:
  7.2 0.8 dynamic_slice.3
  8.0 0.7 fusion.58
  8.7 0.7 fusion.47
  9.4 1.1 fusion.22
  10.6 2.1 pad_add_fusion
  12.6 1.1 fusion.46
  13.8 0.8 bitcast_select_fusion
  14.5 1.3 dynamic-slice
  16.4 110.0 %all-reduce.6.cloned.1.call-done = f32[320,128]{1,0:T(8,128)} async-done(((f32[320,128]{1,0:T(8,128)}), f32[320,128]{1,0:T(8,128)}) %all-reduce.6.cloned.1.call-update) | async-done | bytes 163856
  126.4 0.7 constant_dynamic-slice_fusion.1
  127.2 23.5 %psum.42 = f32[80,16]{1,0:T(8,128)S(1)} all-reduce(f32[80,16]{1,0:T(8,128)S(1)} %reshape.170), channel_id=1, replica_groups=mesh['wide'=32,'narrow'=8] {'narrow'}, use_global_device_ids=true, to_apply=%region_1.0 | all-reduce | flops 1280 | bytes 10240 | tf_op jit(solution)/shard_map/psum | solution.py:73
  151.1 30.1 %all-gather = f32[32,10,128]{2,1,0:T(8,128)S(1)} all-gather(f32[1,10,128]{2,1,0:T(8,128)S(1)} %reshape.179), channel_id=1, replica_groups=mesh['wide'=32,'narrow'=8] {'wide'}, dimensions={0}, use_global_device_ids=true | all-gather | bytes 168960 | tf_op jit(solution)/shard_map/all_gather | solution.py:77
  181.6 1.1 fusion.59
  182.7 1.3 collective-permute-start.1
  184.1 1.2 convert_convert_fusion
  185.3 12.3 %copy.57 = bf16[2048,2048]{1,0:T(8,128)(2,1)} copy(bf16[2048,2048]{0,1:T(8,128)(2,1)} %bitcast.206) | data formatting | bytes 16777216 | tf_op jit(solution)/shard_map/dot_general | solution.py:106
  197.6 2.6 collective-permute-start
  200.4 0.7 collective-permute-done
  201.2 0.4 fusion
  201.7 5.6 fusion.60
  207.8 0.5 fusion.5
  208.3 0.6 fusion.7
  208.9 1.3 collective-permute-start.3
  210.2 1.9 collective-permute-start.2
  212.1 2.1 collective-permute-done.3
  214.2 1.7 collective-permute-done.2
  216.1 78.5 %all-reduce.2 = (f32[16]{0:T(128)S(1)}, f32[16]{0:T(128)S(1)}) all-reduce(f32[16]{0:T(128)S(1)} %get-tuple-element.9, f32[16]{0:T(128)S(1)} %get-tuple-element.8), channel_id=1, replica_groups=mesh['wide'=32,'narrow'=8] {'wide','narrow'}, use_global_device_ids=true, to_apply=%region_3.0 | all-reduce | flops 32 | bytes 256 | tf_op jit(solution)/shard_map/psum | solution.py:81
  295.0 1.1 fusion.44
  296.1 106.8 %all-reduce.8.cloned.1.call-done = f32[320,128]{1,0:T(8,128)} async-done(((f32[320,128]{1,0:T(8,128)}), f32[320,128]{1,0:T(8,128)}) %all-reduce.8.cloned.1.call-update) | async-done | bytes 163856
  402.9 0.7 constant_dynamic-slice_fusion
  403.7 23.5 %psum.45 = f32[80,16]{1,0:T(8,128)S(1)} all-reduce(f32[80,16]{1,0:T(8,128)S(1)} %reshape.175), channel_id=1, replica_groups=mesh['wide'=32,'narrow'=8] {'narrow'}, use_global_device_ids=true, to_apply=%region_7.0 | all-reduce | flops 1280 | bytes 10240 | tf_op jit(solution)/shard_map/psum | solution.py:73
  427.6 30.1 %all-gather.1 = f32[32,10,128]{2,1,0:T(8,128)S(1)} all-gather(f32[1,10,128]{2,1,0:T(8,128)S(1)} %reshape.181), channel_id=1, replica_groups=mesh['wide'=32,'narrow'=8] {'wide'}, dimensions={0}, use_global_device_ids=true | all-gather | bytes 168960 | tf_op jit(solution)/shard_map/all_gather | solution.py:77
  458.1 0.4 multiply_reduce_fusion
  458.5 73.3 %psum.46 = f32[16]{0:T(128)S(1)} all-reduce(f32[16]{0:T(128)S(1)} %get-tuple-element.39), channel_id=1, replica_groups=mesh['wide'=32,'narrow'=8] {'wide','narrow'}, use_global_device_ids=true, to_apply=%region_9.0 | all-reduce | flops 16 | bytes 128 | tf_op jit(solution)/shard_map/psum | solution.py:81
  531.9 2.4 collective-permute-start.4
  534.4 3.9 collective-permute-start.5
  538.4 0.5 collective-permute-done.5
  539.1 0.4 fusion.1
  539.5 5.6 fusion.61
  545.6 0.5 fusion.4
  546.1 0.6 fusion.6
  546.7 1.3 collective-permute-start.7
  548.0 2.7 collective-permute-start.6
  550.8 0.9 collective-permute-done.7
  551.6 1.6 collective-permute-done.6
  553.5 78.3 %psum.47 = f32[16]{0:T(128)S(1)} all-reduce(f32[16]{0:T(128)S(1)} %fusion.15), channel_id=1, replica_groups=mesh['wide'=32,'narrow'=8] {'wide','narrow'}, use_global_device_ids=true, to_apply=%region_11.0 | all-reduce | flops 16 | bytes 128 | tf_op jit(solution)/shard_map/psum | solution.py:118
  631.8 0.7 copy.47
  632.6 0.7 copy.48
  (55 shorter events, 4.3 us)
Async XLA Ops:
  7.2 143.6 %copy-start = (f32[1,80,80]{2,1,0:T(8,128)S(1)}, f32[1,80,80]{2,1,0:T(8,128)}, u32[]{:S(2)}) copy-start(f32[1,80,80]{2,1,0:T(8,128)} %param.13) | copy-start | bytes 76804
  7.2 119.2 %all-reduce.6.cloned.1.call-start = ((), (), s32[]{:S(2)}) async-start(), calls=%async_computation | async-start | bytes 327680
  13.7 389.2 %all-reduce.8.cloned.1.call-start = ((), (), s32[]{:S(2)}) async-start(), calls=%async_computation.1 | async-start | bytes 327680
  182.7 17.5 %collective-permute-start.1 = (bf16[16,512]{1,0:T(8,128)(2,1)S(1)}, bf16[16,512]{1,0:T(8,128)(2,1)S(1)}, u32[]{:S(2)}, u32[]{:S(2)}) collective-permute-start(bf16[16,512]{1,0:T(8,128)(2,1)S(1)} %get-tuple-element.30), channel_id=1, source_target_pairs={{0,1},{1,2},{2,3},{3,4},{4,5},{5,6},{6,7},{8,9},{9,10},{10,11},{11... | collective-permute-start | bytes 49160 | tf_op jit(solution)/shard_map/ppermute | solution.py:13
  185.3 16.0 %copy-start.3 = (s32[1,1,4]{2,1,0:T(1,128)S(1)}, s32[1,1,4]{2,1,0:T(1,128)}, u32[]{:S(2)}) copy-start(s32[1,1,4]{2,1,0:T(1,128)} %param.16) | copy-start | bytes 52
  197.6 18.4 %copy-start.1 = (f32[1,1,16,2,512]{4,3,2,1,0:T(2,128)S(1)}, f32[1,1,16,2,512]{4,3,2,1,0:T(2,128)}, u32[]{:S(2)}) copy-start(f32[1,1,16,2,512]{4,3,2,1,0:T(2,128)} %param.9) | copy-start | bytes 196612
  197.6 97.1 %copy-start.2 = (f32[1,1,2,2,8,512]{5,4,3,2,1,0:T(8,128)S(1)}, f32[1,1,2,2,8,512]{5,4,3,2,1,0:T(8,128)}, u32[]{:S(2)}) copy-start(f32[1,1,2,2,8,512]{5,4,3,2,1,0:T(8,128)} %param.12) | copy-start | bytes 196612
  197.6 3.4 collective-permute-start
  208.9 5.4 collective-permute-start.3
  210.2 5.8 collective-permute-start.2
  531.9 6.3 collective-permute-start.4
  534.4 4.5 collective-permute-start.5
  546.7 4.9 collective-permute-start.7
  548.0 5.2 collective-permute-start.6
Sparse Core Ops, SparseCore 0:
  13.8 112.5 all-reduce.5
  296.3 106.6 all-reduce.7
where the time goes:
time: 641 us; the launch traced here: 640 us
  blocking collectives  337 us (53%)
  waiting for transfers between devices  224 us (35%)
  matrix products  21.5 us (3%)
  local copies, waits for them, and re-layouts  18.9 us (3%)
  starting transfers between devices  17.5 us (3%)
  between operations  15 us (2%)
    unnamed x4, waiting for transfers between devices  217 us
    psum x2, blocking collectives, precondition(): lax.psum(jnp.sum(residual * precond, axis=(1, 2)), ('wide', 'narrow'))  152 us
    psum x1, blocking collectives, body(): lax.psum(jnp.sum(direction * applied, axis=(1, 2)), ('wide', 'narrow'))  78.3 us
    all_gather x2, blocking collectives, precondition(): lax.all_gather(solved.reshape(capacity, basis_count * nrhs_count), 'wide'...  60.2 us
    psum x2, blocking collectives, precondition(): lax.psum(owned_rows, 'narrow').reshape(block_order, nrhs_count)  47.1 us
    ppermute x8, starting transfers between devices, shifted(): return lax.ppermute(block, axis, route)  17.5 us
  transfers between devices with their start and end apart: 10, of which 8 were waited for; matrix products, arithmetic and copies ran while one was open for 2% of the time, Pallas kernels for 0%

commit v1 on v0

--- a/solution.py
+++ b/solution.py
@@ -74,9 +74,9 @@
         solved = jnp.dot(
             inverse_block, owner_block, precision=highest, preferred_element_type=jnp.float32
         )
-        all_solved = lax.all_gather(
-            solved.reshape(capacity, basis_count * nrhs_count), "wide", axis=0, tiled=True
-        )
+        block_2 = solved.reshape(capacity, basis_count * nrhs_count)
+        sent = jnp.stack([block_2] * lax.axis_size("wide"))
+        all_solved = jnp.concatenate(lax.all_to_all(sent, "wide", 0, 0), axis=0)
         precond = finish(residual, all_solved)
         inner_value = lax.psum(jnp.sum(residual * precond, axis=(1, 2)), ("wide", "narrow"))
         return (precond, inner_value)

time: 641 us -> 622 us (0.970)
  blocking collectives: 337 us -> 296 us
  starting transfers between devices: 17.5 us -> 28.3 us
  waiting for transfers between devices: 224 us -> 233 us
    all_gather x2 -> x0, blocking collectives: 60.2 us -> none  [precondition(): lax.all_gather(solved.reshape(capacity, basis_count * nrhs_count), 'wide'...]
    all_to_all x0 -> x1, blocking collectives: none -> 19.7 us  [precondition(): all_solved = jnp.concatenate(lax.all_to_all(sent, 'wide', 0, 0), axis=0)]
    all_to_all x0 -> x1, starting transfers between devices: none -> 10.9 us  [precondition(): all_solved = jnp.concatenate(lax.all_to_all(sent, 'wide', 0, 0), axis=0)]
    all_to_all x0 -> x1, waiting for transfers between devices: none -> 8.18 us  [precondition(): all_solved = jnp.concatenate(lax.all_to_all(sent, 'wide', 0, 0), axis=0)]
  transfers between devices with their start and end apart: 10 -> 11, of which waited for: 8 -> 9; matrix products, arithmetic and copies ran while one was open for 2% -> 3% of each run, Pallas kernels for 0% -> 0%
where the time goes in v1:
time: 622 us; the launch traced here: 621 us
  blocking collectives  296 us (48%)
  waiting for transfers between devices  233 us (37%)
  starting transfers between devices  28.3 us (5%)
  matrix products  22.4 us (4%)
  local copies, waits for them, and re-layouts  19.8 us (3%)
  between operations  15 us (2%)
    unnamed x4, waiting for transfers between devices  218 us
    psum x2, blocking collectives, precondition(): lax.psum(jnp.sum(residual * precond, axis=(1, 2)), ('wide', 'narrow'))  152 us
    psum x1, blocking collectives, body(): lax.psum(jnp.sum(direction * applied, axis=(1, 2)), ('wide', 'narrow'))  78.1 us
    psum x2, blocking collectives, precondition(): lax.psum(owned_rows, 'narrow').reshape(block_order, nrhs_count)  47.1 us
    all_to_all x1, blocking collectives, precondition(): all_solved = jnp.concatenate(lax.all_to_all(sent, 'wide', 0, 0), axis=0)  19.7 us
    ppermute x8, starting transfers between devices, shifted(): return lax.ppermute(block, axis, route)  17.3 us
  transfers between devices with their start and end apart: 11, of which 9 were waited for; matrix products, arithmetic and copies ran while one was open for 3% of the time, Pallas kernels for 0%

profile of v1, /device:TPU:1, one launch (start us, length us, event | category | flops | bytes accessed | tf_op | source)
XLA Modules:
  0.0 620.8 jit_solution(16055537913704447579)
XLA Ops:
  7.2 0.8 dynamic_slice.3
  8.0 0.7 fusion.62
  8.7 0.7 fusion.51
  9.4 1.1 fusion.22
  10.6 2.1 pad_add_fusion
  12.6 1.1 fusion.50
  13.8 1.3 dynamic-slice
  15.7 110.7 %all-reduce.6.cloned.1.call-done = f32[320,128]{1,0:T(8,128)} async-done(((f32[320,128]{1,0:T(8,128)}), f32[320,128]{1,0:T(8,128)}) %all-reduce.6.cloned.1.call-update) | async-done | bytes 163856
  126.4 0.7 constant_dynamic-slice_fusion.1
  127.2 23.5 %psum.42 = f32[80,16]{1,0:T(8,128)S(1)} all-reduce(f32[80,16]{1,0:T(8,128)S(1)} %reshape.208), channel_id=1, replica_groups=mesh['wide'=32,'narrow'=8] {'narrow'}, use_global_device_ids=true, to_apply=%region_1.0 | all-reduce | flops 1280 | bytes 10240 | tf_op jit(solution)/shard_map/psum | solution.py:73
  151.1 0.7 stack.62
  151.9 10.9 %all-to-all-start = ((f32[32,10,128]{2,1,0:T(8,128)}), f32[32,10,128]{2,1,0:T(8,128)S(1)}, u32[]{:S(2)}, u32[]{:S(2)}) async-start(f32[32,10,128]{2,1,0:T(8,128)} %stack.62), calls=%async_computation | async-start | bytes 524288 | tf_op jit(solution)/shard_map/all_to_all | solution.py:79
  162.8 0.8 bitcast_select_fusion
  163.6 8.2 %all-to-all-done = f32[32,10,128]{2,1,0:T(8,128)S(1)} async-done(((f32[32,10,128]{2,1,0:T(8,128)}), f32[32,10,128]{2,1,0:T(8,128)S(1)}, u32[]{:S(2)}, u32[]{:S(2)}) %all-to-all-start) | async-done | bytes 163872 | tf_op jit(solution)/shard_map/all_to_all | solution.py:79
  171.9 0.6 fusion.47
  172.5 1.2 fusion.63
  173.7 1.3 collective-permute-start.1
  175.0 1.2 convert_convert_fusion
  176.2 12.3 %copy.64 = bf16[2048,2048]{1,0:T(8,128)(2,1)} copy(bf16[2048,2048]{0,1:T(8,128)(2,1)} %bitcast.220) | data formatting | bytes 16777216 | tf_op jit(solution)/shard_map/dot_general | solution.py:106
  188.5 2.3 collective-permute-start
  191.0 0.7 collective-permute-done
  192.4 5.6 fusion.64
  198.5 0.5 fusion.5
  199.0 0.6 fusion.7
  199.6 1.3 collective-permute-start.3
  200.9 2.1 collective-permute-start.2
  202.9 1.4 collective-permute-done.3
  204.4 2.3 collective-permute-done.2
  206.8 78.8 %all-reduce.2 = (f32[16]{0:T(128)S(1)}, f32[16]{0:T(128)S(1)}) all-reduce(f32[16]{0:T(128)S(1)} %get-tuple-element.9, f32[16]{0:T(128)S(1)} %get-tuple-element.8), channel_id=1, replica_groups=mesh['wide'=32,'narrow'=8] {'wide','narrow'}, use_global_device_ids=true, to_apply=%region_3.0 | all-reduce | flops 32 | bytes 256 | tf_op jit(solution)/shard_map/psum | solution.py:81
  285.9 1.1 fusion.49
  287.0 106.9 %all-reduce.8.cloned.1.call-done = f32[320,128]{1,0:T(8,128)} async-done(((f32[320,128]{1,0:T(8,128)}), f32[320,128]{1,0:T(8,128)}) %all-reduce.8.cloned.1.call-update) | async-done | bytes 163856
  394.0 0.7 constant_dynamic-slice_fusion
  394.8 23.5 %psum.45 = f32[80,16]{1,0:T(8,128)S(1)} all-reduce(f32[80,16]{1,0:T(8,128)S(1)} %reshape.212), channel_id=1, replica_groups=mesh['wide'=32,'narrow'=8] {'narrow'}, use_global_device_ids=true, to_apply=%region_7.0 | all-reduce | flops 1280 | bytes 10240 | tf_op jit(solution)/shard_map/psum | solution.py:73
  418.7 19.7 %all_to_all.10 = f32[32,10,128]{2,1,0:T(8,128)S(1)} all-to-all(f32[32,10,128]{2,1,0:T(8,128)S(1)} %stack.69), channel_id=1, replica_groups=mesh['wide'=32,'narrow'=8] {'wide'}, dimensions={0} | all-to-all | bytes 327680 | tf_op jit(solution)/shard_map/all_to_all | solution.py:79
  438.6 0.6 fusion.45
  439.6 72.9 %psum.46 = f32[16]{0:T(128)S(1)} all-reduce(f32[16]{0:T(128)S(1)} %get-tuple-element.39), channel_id=1, replica_groups=mesh['wide'=32,'narrow'=8] {'wide','narrow'}, use_global_device_ids=true, to_apply=%region_9.0 | all-reduce | flops 16 | bytes 128 | tf_op jit(solution)/shard_map/psum | solution.py:81
  512.6 2.6 collective-permute-start.4
  515.2 3.9 collective-permute-start.5
  520.4 5.6 fusion.65
  526.5 0.5 fusion.4
  527.0 0.6 fusion.6
  527.6 1.3 collective-permute-start.7
  528.9 2.6 collective-permute-start.6
  531.4 1.1 collective-permute-done.7
  532.5 1.6 collective-permute-done.6
  534.3 78.1 %psum.47 = f32[16]{0:T(128)S(1)} all-reduce(f32[16]{0:T(128)S(1)} %fusion.15), channel_id=1, replica_groups=mesh['wide'=32,'narrow'=8] {'wide','narrow'}, use_global_device_ids=true, to_apply=%region_11.0 | all-reduce | flops 16 | bytes 128 | tf_op jit(solution)/shard_map/psum | solution.py:118
  612.5 0.7 copy.53
  613.3 0.7 copy.54
  (59 shorter events, 5.8 us)
Async XLA Ops:
  7.2 143.6 %copy-start = (f32[1,80,80]{2,1,0:T(8,128)S(1)}, f32[1,80,80]{2,1,0:T(8,128)}, u32[]{:S(2)}) copy-start(f32[1,80,80]{2,1,0:T(8,128)} %param.13) | copy-start | bytes 76804
  7.2 119.2 %all-reduce.6.cloned.1.call-start = ((), (), s32[]{:S(2)}) async-start(), calls=%async_computation.2 | async-start | bytes 327680
  151.9 19.9 %all-to-all-start = ((f32[32,10,128]{2,1,0:T(8,128)}), f32[32,10,128]{2,1,0:T(8,128)S(1)}, u32[]{:S(2)}, u32[]{:S(2)}) async-start(f32[32,10,128]{2,1,0:T(8,128)} %stack.62), calls=%async_computation | async-start | bytes 524288 | tf_op jit(solution)/shard_map/all_to_all | solution.py:79
  162.8 231.2 %all-reduce.8.cloned.1.call-start = ((), (), s32[]{:S(2)}) async-start(), calls=%async_computation.3 | async-start | bytes 327680
  173.7 17.2 %collective-permute-start.1 = (bf16[16,512]{1,0:T(8,128)(2,1)S(1)}, bf16[16,512]{1,0:T(8,128)(2,1)S(1)}, u32[]{:S(2)}, u32[]{:S(2)}) collective-permute-start(bf16[16,512]{1,0:T(8,128)(2,1)S(1)} %get-tuple-element.30), channel_id=1, source_target_pairs={{0,1},{1,2},{2,3},{3,4},{4,5},{5,6},{6,7},{8,9},{9,10},{10,11},{11... | collective-permute-start | bytes 49160 | tf_op jit(solution)/shard_map/ppermute | solution.py:13
  176.2 15.7 %copy-start.3 = (s32[1,1,4]{2,1,0:T(1,128)S(1)}, s32[1,1,4]{2,1,0:T(1,128)}, u32[]{:S(2)}) copy-start(s32[1,1,4]{2,1,0:T(1,128)} %param.16) | copy-start | bytes 52
  188.5 18.1 %copy-start.1 = (f32[1,1,16,2,512]{4,3,2,1,0:T(2,128)S(1)}, f32[1,1,16,2,512]{4,3,2,1,0:T(2,128)}, u32[]{:S(2)}) copy-start(f32[1,1,16,2,512]{4,3,2,1,0:T(2,128)} %param.9) | copy-start | bytes 196612
  188.5 97.0 %copy-start.2 = (f32[1,1,2,2,8,512]{5,4,3,2,1,0:T(8,128)S(1)}, f32[1,1,2,2,8,512]{5,4,3,2,1,0:T(8,128)}, u32[]{:S(2)}) copy-start(f32[1,1,2,2,8,512]{5,4,3,2,1,0:T(8,128)} %param.12) | copy-start | bytes 196612
  188.5 3.2 collective-permute-start
  199.6 4.8 collective-permute-start.3
  200.9 5.7 collective-permute-start.2
  512.6 6.5 %collective-permute-start.4 = (bf16[16,512]{1,0:T(8,128)(2,1)S(1)}, bf16[16,512]{1,0:T(8,128)(2,1)S(1)}, u32[]{:S(2)}, u32[]{:S(2)}) collective-permute-start(bf16[16,512]{1,0:T(8,128)(2,1)S(1)} %get-tuple-element.25), channel_id=1, source_target_pairs={{0,8},{8,16},{16,24},{24,32},{32,40},{40,48},{48,56},{56,64},{64,7... | collective-permute-start | bytes 49160 | tf_op jit(solution)/shard_map/ppermute | solution.py:13
  515.2 4.5 collective-permute-start.5
  527.6 4.9 collective-permute-start.7
  528.9 5.2 collective-permute-start.6
Sparse Core Ops, SparseCore 0:
  13.8 112.5 all-reduce.5
  287.2 106.7 all-reduce.7
